TPU v7x, 32 devices: a whole 2x2x4 slice. The times are simulated.
32 devices in a mesh: row: 4 (over x, core), col: 8 (over z, y).
Axes of the slice: x: 2, y: 2, z: 4, core: 2. Of those that a mesh axis runs over, the one named last changes fastest.
Arguments:
- features: bfloat16 [4096, 256], P(('row', 'col')), may hold values from -192 to 192
- grad_out: bfloat16 [4096, 256], P(('row', 'col')), may hold values from -192 to 192
- tile_weight: bfloat16 [2048, 128, 128], P(('row', 'col')), may hold values from 0 to 256, as said below
- tile_list: int32 [128, 3, 32], P(('row', 'col')), may hold values from -1 to 63, as said below
Outputs:
- aggregated: bfloat16 [4096, 256], P(('row', 'col'))
- feature_grad: bfloat16 [4096, 256], P(('row', 'col'))
Inputs may be any that keep to these rules, and one draw needn't show every extreme that they name: `tile_list`: each column of a list is a slot (tile number, source block below 1, destination block below 8); tile number -1 marks an empty slot, whose blocks are 0. The tile numbers listed by one device are distinct and are 0 to n - 1 for some n between 40 and 64; some device lists all 64. On every device some step has all 32 slots used. Stored tiles that no slot lists take no part. `tile_weight`: entries are whole numbers.
All inputs are finite; a program needn't handle non-finite values.
Results may differ from a plain program's by a relative error of at most 0.017.
Values may be sent and summed in bfloat16 or wider, within the bound.
No kernel may reach another device: no remote copies, remote signals or barrier semaphores. Data moves between devices by JAX's collectives and lax.ppermute only.
A program may use at most 64 MiB of HBM per device.

v0:
```python
import math
import jax
import jax.numpy as jnp
from jax import lax
from jax.sharding import PartitionSpec as P


def passed_along(value, axis, steps):
    count = lax.axis_size(axis)
    pairs = [(source, (source + steps) % count) for source in range(count)]
    return lax.ppermute(value, axis, pairs)


def local(features, grad_out, tile_weight, tile_list):
    step_count = lax.axis_size("row")
    columns = lax.axis_size("col")
    row_pos = lax.axis_index("row")
    slot_count = tile_list.shape[2]
    tiles_here = tile_weight.shape[0]
    tile_len = tile_weight.shape[1]
    feat_width = features.shape[1]
    src_blocks = features.shape[0] // tile_len
    dst_blocks = columns * (grad_out.shape[0] // tile_len)
    flat_ids = tile_list[:, 0, :].reshape(-1)
    flat_step = jnp.arange(step_count * slot_count, dtype=jnp.int32) // slot_count
    matches = (flat_ids[None, :] == jnp.arange(tiles_here, dtype=jnp.int32)[:, None]).astype(
        jnp.int32
    )
    tile_used = jnp.sum(matches, axis=1)
    tile_step = jnp.sum(matches * flat_step[None, :], axis=1)
    tile_src = jnp.sum(matches * tile_list[:, 1, :].reshape(-1)[None, :], axis=1)
    tile_dst = jnp.sum(matches * tile_list[:, 2, :].reshape(-1)[None, :], axis=1)
    owner_row = (row_pos - tile_step) % step_count
    src_slot = owner_row * src_blocks + tile_src
    used_float = tile_used.astype(jnp.float32)
    row_sums = jnp.sum(tile_weight, axis=2, dtype=jnp.float32)
    col_sums = jnp.sum(tile_weight, axis=1, dtype=jnp.float32)
    dst_pick = (tile_dst[:, None] == jnp.arange(dst_blocks, dtype=jnp.int32)[None, :]).astype(
        jnp.float32
    ) * used_float[:, None]
    src_pick = (
        src_slot[:, None] == jnp.arange(step_count * src_blocks, dtype=jnp.int32)[None, :]
    ).astype(jnp.float32) * used_float[:, None]
    dst_terms = jnp.dot(dst_pick.T, row_sums, precision=lax.Precision.HIGHEST).reshape(-1)
    src_terms = jnp.dot(src_pick.T, col_sums, precision=lax.Precision.HIGHEST).reshape(-1)
    src_scale = lax.rsqrt(1.0 + lax.psum_scatter(src_terms, "row", scatter_dimension=0, tiled=True))
    dst_scale = lax.rsqrt(1.0 + lax.psum_scatter(dst_terms, "col", scatter_dimension=0, tiled=True))
    scaled = (features.astype(jnp.float32) * src_scale[:, None]).astype(jnp.bfloat16)
    scaled = scaled.reshape(src_blocks, tile_len, feat_width)
    scaled_grads = (grad_out.astype(jnp.float32) * dst_scale[:, None]).astype(jnp.bfloat16)
    grad_rows = lax.all_gather(scaled_grads, "col", axis=0, tiled=True).reshape(
        dst_blocks, tile_len, feat_width
    )

    def pick_tiles(list_step):
        tile_ids = tile_list[list_step, 0]
        keep_mask = (tile_ids >= 0).astype(jnp.bfloat16)
        chosen = tile_weight[jnp.maximum(tile_ids, 0)] * keep_mask[:, None, None]
        return (chosen, tile_list[list_step, 1], tile_list[list_step, 2])

    def backward_add(accum_total, rows, list_step):
        chosen, src_index, dst_index = pick_tiles(list_step)
        products = jnp.einsum(
            "kij,kif->kjf", chosen, rows[dst_index], preferred_element_type=jnp.float32
        )
        return accum_total.at[src_index].add(products)

    def grad_step(grad_state, step_pos):
        return backward_add(grad_state, grad_rows, step_count - 1 - step_pos)

    def grad_move(grad_state):
        return passed_along(grad_state.astype(jnp.bfloat16), "row", -1).astype(grad_state.dtype)

    partial_zero = jnp.zeros((dst_blocks, tile_len, feat_width), jnp.float32)
    everything = lax.all_gather(scaled, "row", axis=0, tiled=True)
    batch_size = math.gcd(tiles_here, 16)

    def tile_batch(loop_index, partial_value):
        first_tile = loop_index * batch_size
        tile_block = lax.dynamic_slice_in_dim(tile_weight, first_tile, batch_size, 0)
        keep_mask = lax.dynamic_slice_in_dim(tile_used, first_tile, batch_size, 0).astype(
            jnp.bfloat16
        )
        src_index = lax.dynamic_slice_in_dim(src_slot, first_tile, batch_size, 0)
        dst_index = lax.dynamic_slice_in_dim(tile_dst, first_tile, batch_size, 0)
        chosen = tile_block * keep_mask[:, None, None]
        products = jnp.einsum(
            "kij,kjf->kif", chosen, everything[src_index], preferred_element_type=jnp.float32
        )
        return partial_value.at[dst_index].add(products)

    partial_value = lax.fori_loop(0, tiles_here // batch_size, tile_batch, partial_zero)

    def grad_loop(step_pos, grad_state):
        return grad_move(grad_step(grad_state, step_pos))

    grad_state = lax.fori_loop(
        0, step_count - 1, grad_loop, jnp.zeros((src_blocks, tile_len, feat_width), jnp.float32)
    )
    grad_state = grad_step(grad_state, step_count - 1)
    summed = lax.psum_scatter(
        partial_value.reshape(dst_blocks * tile_len, feat_width).astype(jnp.bfloat16),
        "col",
        scatter_dimension=0,
        tiled=True,
    ).astype(jnp.float32)
    aggregated = (summed * dst_scale[:, None]).astype(jnp.bfloat16)
    grads = grad_state.reshape(src_blocks * tile_len, feat_width)
    feature_grad = (grads * src_scale[:, None]).astype(jnp.bfloat16)
    return (aggregated, feature_grad)


def solution(mesh):
    return jax.shard_map(
        local,
        mesh=mesh,
        in_specs=(
            P(("row", "col"), None),
            P(("row", "col"), None),
            P(("row", "col"), None, None),
            P(("row", "col"), None, None),
        ),
        out_specs=(P(("row", "col"), None), P(("row", "col"), None)),
        check_vma=False,
    )
```

profile of v0, /device:TPU:0, one launch (start us, length us, event | category | flops | bytes accessed | tf_op | source)
XLA Modules:
  0.0 244.0 jit_solution(11328118093270040016)
XLA Ops:
  7.2 0.8 fusion.26
  8.1 0.7 fusion.27
  8.8 0.7 fusion.29
  10.1 0.7 fusion.34
  10.8 0.7 copy.13
  11.5 1.3 dynamic-slice.2
  12.9 1.2 dynamic-slice
  15.8 2.3 convert_reduce_fusion
  18.3 8.4 %all-reduce = f32[512]{0:T(512)S(1)} all-reduce(f32[512]{0:T(512)S(1)} %convolution_bitcast_fusion.1), channel_id=3, replica_groups=mesh['row'=4,'col'=8] {'row'}, use_global_device_ids=true, to_apply=%region_5.6.clone | all-reduce | flops 512 | bytes 4096
  26.9 21.7 %all-reduce.1 = f32[1024]{0:T(1024)S(1)} all-reduce(f32[1024]{0:T(1024)S(1)} %convolution_bitcast_fusion), channel_id=5, replica_groups=mesh['row'=4,'col'=8] {'col'}, use_global_device_ids=true, to_apply=%region_11.12.clone | all-reduce | flops 1024 | bytes 8192
  48.8 31.5 %all_gather.7 = bf16[1024,256]{1,0:T(8,128)(2,1)S(1)} all-gather(bf16[128,256]{1,0:T(8,128)(2,1)S(1)} %multiply_convert_fusion), channel_id=1, replica_groups=mesh['row'=4,'col'=8] {'col'}, dimensions={0}, use_global_device_ids=true | all-gather | bytes 589824 | tf_op jit(solution)/shard_map/all_gather | solution.py:51
  80.3 1.7 gather_fusion.3
  82.1 2.0 gather_fusion.4
  84.1 5.0 %fusion.13 = f32[32,128,256]{2,1,0:T(8,128)} fusion(bf16[32,128,256]{2,1,0:T(8,128)(2,1)} %gather_fusion.4, bf16[32,128,128]{2,1,0:T(8,128)(2,1)} %gather_fusion.3, bf16[32]{0:T(256)(128)(2,1)S(1)} %fusion.26), kind=kOutput, calls=%fused_computation.41 | convolution fusion | flops 268959744 | bytes 7340096 | tf_op jit(solution)/shard_map/kij,kif->kjf/dot_general | solution.py:63
  89.0 49.5 %while.30 = (s32[]{:T(128)}, f32[1,128,256]{2,1,0:T(8,128)S(1)}, s32[4,3,32]{2,1,0:T(4,128)S(1)}, bf16[64,128,128]{2,1,0:T(8,128)(2,1)S(1)}, bf16[8,128,256]{2,1...) while((s32[]{:T(128)}, f32[1,128,256]{2,1,0:T(8,128)S(1)}, ...), condition=%wide.region_14.15_spmd.clone, body=%wide.region_12.14_spmd.clone.sunk | while | flops 270109056 | bytes 35530608 | solution.py:97
  89.1 1.7 gather_fusion.2
  91.6 4.3 %fusion.57 = f32[32,128,256]{2,1,0:T(8,128)} fusion(bf16[32,128,256]{2,1,0:T(8,128)(2,1)S(1)} %gather_fusion.1, bf16[32,128,128]{2,1,0:T(8,128)(2,1)} %gather_fusion.2, bf16[32]{0:T(256)(128)(2,1)S(1)} %fusion.56), kind=kOutput, calls=%fused_computation.17.clone.1 | convolution fusion | flops 268959744 | bytes 7340096 | tf_op jit(solution)/shard_map/while/body/eval_jaxpr/kij,kif->kjf/dot_general | solution.py:63
  95.9 6.4 %scatter_fusion.1 = f32[128,256,1]{1,0,2:T(8,128)S(1)} fusion(f32[128,256,1]{1,0,2:T(8,128)S(1)} %select_bitcast_fusion.2, s32[32]{0:T(128)S(1)} %fusion.54, f32[32,128,256]{2,1,0:T(8,128)} %fusion.57), kind=kCustom, calls=%fused_computation.6.clone.clone.1 | custom fusion | flops 1048576 | bytes 12583040 | tf_op jit(solution)/shard_map/while/body/eval_jaxpr/scatter-add | solution.py:66
  102.4 1.9 collective-permute-done
  104.5 1.7 gather_fusion.2
  106.9 4.3 %fusion.57 = f32[32,128,256]{2,1,0:T(8,128)} fusion(bf16[32,128,256]{2,1,0:T(8,128)(2,1)S(1)} %gather_fusion.1, bf16[32,128,128]{2,1,0:T(8,128)(2,1)} %gather_fusion.2, bf16[32]{0:T(256)(128)(2,1)S(1)} %fusion.56), kind=kOutput, calls=%fused_computation.17.clone.1 | convolution fusion | flops 268959744 | bytes 7340096 | tf_op jit(solution)/shard_map/while/body/eval_jaxpr/kij,kif->kjf/dot_general | solution.py:63
  111.2 6.4 %scatter_fusion.1 = f32[128,256,1]{1,0,2:T(8,128)S(1)} fusion(f32[128,256,1]{1,0,2:T(8,128)S(1)} %select_bitcast_fusion.2, s32[32]{0:T(128)S(1)} %fusion.54, f32[32,128,256]{2,1,0:T(8,128)} %fusion.57), kind=kCustom, calls=%fused_computation.6.clone.clone.1 | custom fusion | flops 1048576 | bytes 12583040 | tf_op jit(solution)/shard_map/while/body/eval_jaxpr/scatter-add | solution.py:66
  117.7 1.8 collective-permute-start
  119.5 1.9 collective-permute-done
  121.6 1.7 gather_fusion.2
  124.0 4.3 %fusion.57 = f32[32,128,256]{2,1,0:T(8,128)} fusion(bf16[32,128,256]{2,1,0:T(8,128)(2,1)S(1)} %gather_fusion.1, bf16[32,128,128]{2,1,0:T(8,128)(2,1)} %gather_fusion.2, bf16[32]{0:T(256)(128)(2,1)S(1)} %fusion.56), kind=kOutput, calls=%fused_computation.17.clone.1 | convolution fusion | flops 268959744 | bytes 7340096 | tf_op jit(solution)/shard_map/while/body/eval_jaxpr/kij,kif->kjf/dot_general | solution.py:63
  128.3 6.4 %scatter_fusion.1 = f32[128,256,1]{1,0,2:T(8,128)S(1)} fusion(f32[128,256,1]{1,0,2:T(8,128)S(1)} %select_bitcast_fusion.2, s32[32]{0:T(128)S(1)} %fusion.54, f32[32,128,256]{2,1,0:T(8,128)} %fusion.57), kind=kCustom, calls=%fused_computation.6.clone.clone.1 | custom fusion | flops 1048576 | bytes 12583040 | tf_op jit(solution)/shard_map/while/body/eval_jaxpr/scatter-add | solution.py:66
  134.8 1.8 collective-permute-start
  136.6 1.9 collective-permute-done
  138.6 6.3 %scatter_fusion.2 = f32[128,256,1]{1,0,2:T(8,128)S(1)} fusion(f32[128,256,1]{1,0,2:T(8,128)S(1)} %bitcast.83, s32[32]{0:T(128)S(1)} %fusion.27, f32[32,128,256]{2,1,0:T(8,128)} %fusion.13), kind=kCustom, calls=%fused_computation.7 | custom fusion | flops 1048576 | bytes 12583040 | tf_op jit(solution)/shard_map/scatter-add | solution.py:66
  144.9 0.7 fusion.16
  145.6 6.0 %all-gather = bf16[512,256]{1,0:T(8,128)(2,1)S(1)} all-gather(bf16[128,256]{1,0:T(8,128)(2,1)S(1)} %get-tuple-element.329), channel_id=2, replica_groups=mesh['row'=4,'col'=8] {'row'}, dimensions={0}, use_global_device_ids=true | all-gather | bytes 327680 | tf_op jit(solution)/shard_map/all_gather | solution.py:75
  151.7 23.5 %while.29 = (s32[]{:T(128)}, f32[8,128,256]{2,1,0:T(8,128)S(1)}, s32[64]{0:T(128)S(1)}, bf16[64,128,128]{2,1,0:T(8,128)(2,1)}, s32[64]{0:T(128)S(1)}, /*index=5*...) while((s32[]{:T(128)}, f32[8,128,256]{2,1,0:T(8,128)S(1)}, ...), condition=%wide.region_8.9_spmd, body=%wide.region_6.8_spmd.sunk | while | flops 135005296 | bytes 12063463 | solution.py:92
  151.9 1.6 gather_fusion
  153.5 1.9 fusion.51
  155.4 2.2 scatter_fusion
  157.7 1.6 gather_fusion
  159.3 1.9 fusion.51
  161.2 2.2 scatter_fusion
  163.6 1.6 gather_fusion
  165.2 1.9 fusion.51
  167.1 2.2 scatter_fusion
  169.5 1.6 gather_fusion
  171.1 1.9 fusion.51
  173.0 2.2 scatter_fusion
  175.2 0.8 convert_element_type.102
  176.0 59.6 %reduce-scatter.2.cloned.1.call-done = bf16[128,256]{1,0:T(8,128)(2,1)} async-done(((bf16[1024,256]{1,0:T(8,128)(2,1)}), bf16[128,256]{1,0:T(8,128)(2,1)}) %reduce-scatter.2.cloned.1.call-update) | async-done | bytes 65552 | tf_op jit(solution)/shard_map/reduce_scatter | solution.py:101
  235.6 1.6 multiply_convert_fusion.1
  (74 shorter events, 5.1 us)
Async XLA Ops:
  7.2 73.1 %copy-start = (bf16[64,128,128]{2,1,0:T(8,128)(2,1)S(1)}, bf16[64,128,128]{2,1,0:T(8,128)(2,1)}, u32[]{:S(2)}) copy-start(bf16[64,128,128]{2,1,0:T(8,128)(2,1)} %param.10) | copy-start | bytes 6291460
  7.2 41.5 %copy-start.3 = (bf16[128,256]{1,0:T(8,128)(2,1)S(1)}, bf16[128,256]{1,0:T(8,128)(2,1)}, u32[]{:S(2)}) copy-start(bf16[128,256]{1,0:T(8,128)(2,1)} %param.9) | copy-start | bytes 196612
  7.2 228.4 %reduce-scatter.2.cloned.1.call-start = ((), (), s32[]{:S(2)}) async-start(), calls=%async_computation.1 | async-start | bytes 589824 | tf_op jit(solution)/shard_map/reduce_scatter | solution.py:101
  95.9 8.4 %copy-start.1 = (bf16[64,128,128]{2,1,0:T(8,128)(2,1)S(1)}, bf16[64,128,128]{2,1,0:T(8,128)(2,1)}, u32[]{:S(2)}) copy-start(bf16[64,128,128]{2,1,0:T(8,128)(2,1)} %get-tuple-element.478) | copy-start | bytes 6291460 | tf_op jit(solution)/shard_map/while
  102.3 2.0 collective-permute-start
  111.2 10.2 %copy-start.1 = (bf16[64,128,128]{2,1,0:T(8,128)(2,1)S(1)}, bf16[64,128,128]{2,1,0:T(8,128)(2,1)}, u32[]{:S(2)}) copy-start(bf16[64,128,128]{2,1,0:T(8,128)(2,1)} %get-tuple-element.478) | copy-start | bytes 6291460 | tf_op jit(solution)/shard_map/while
  117.7 3.7 %collective-permute-start = (bf16[1,128,256]{2,1,0:T(8,128)(2,1)S(1)}, bf16[1,128,256]{2,1,0:T(8,128)(2,1)S(1)}, u32[]{:S(2)}, u32[]{:S(2)}) collective-permute-start(bf16[1,128,256]{2,1,0:T(8,128)(2,1)S(1)} %convert_bitcast_fusion.2), channel_id=1, source_target_pairs={{0,24},{8,0},{16,8},{24,16},{1,25},{9,1},{17,9},{25,17},{2,26},{10... | collective-permute-start | bytes 196616 | tf_op jit(solution)/shard_map/while/body/eval_jaxpr/ppermute | solution.py:11
  128.3 10.2 %copy-start.1 = (bf16[64,128,128]{2,1,0:T(8,128)(2,1)S(1)}, bf16[64,128,128]{2,1,0:T(8,128)(2,1)}, u32[]{:S(2)}) copy-start(bf16[64,128,128]{2,1,0:T(8,128)(2,1)} %get-tuple-element.478) | copy-start | bytes 6291460 | tf_op jit(solution)/shard_map/while
  134.8 3.7 %collective-permute-start = (bf16[1,128,256]{2,1,0:T(8,128)(2,1)S(1)}, bf16[1,128,256]{2,1,0:T(8,128)(2,1)S(1)}, u32[]{:S(2)}, u32[]{:S(2)}) collective-permute-start(bf16[1,128,256]{2,1,0:T(8,128)(2,1)S(1)} %convert_bitcast_fusion.2), channel_id=1, source_target_pairs={{0,24},{8,0},{16,8},{24,16},{1,25},{9,1},{17,9},{25,17},{2,26},{10... | collective-permute-start | bytes 196616 | tf_op jit(solution)/shard_map/while/body/eval_jaxpr/ppermute | solution.py:11
  138.6 6.4 %copy-start.2 = (bf16[128,256]{1,0:T(8,128)(2,1)S(1)}, bf16[128,256]{1,0:T(8,128)(2,1)}, u32[]{:S(2)}) copy-start(bf16[128,256]{1,0:T(8,128)(2,1)} %param.8) | copy-start | bytes 196612
Sparse Core Ops, SparseCore 0:
  176.1 59.4 reduce-scatter.1
where the time goes:
time: 245 us; the launch traced here: 244 us
  blocking collectives  67.5 us (28%)
  waiting for transfers between devices  65.3 us (27%)
  other arithmetic  43.9 us (18%)
  matrix products  25.9 us (11%)
  local copies, waits for them, and re-layouts  21.7 us (9%)
  between operations  15.4 us (6%)
  starting transfers between devices  3.77 us (2%)
    reduce_scatter x1, waiting for transfers between devices, local(): lax.psum_scatter(partial_value.reshape(dst_blocks * tile_len, feat_width)...  59.6 us
    all_gather x1, blocking collectives, local(): lax.all_gather(scaled_grads, 'col', axis=0, tiled=True)  31.5 us
    unnamed x2, blocking collectives  30 us
    scatter-add x4, other arithmetic, backward_add(): return accum_total.at[src_index].add(products)  25.6 us
    dot_general x4, matrix products, backward_add(): jnp.einsum('kij,kif->kjf', chosen, rows[dst_index], preferred_element_typ...  17.9 us
    scatter-add x4, other arithmetic, tile_batch(): return partial_value.at[dst_index].add(products)  8.78 us
    dot_general x4, matrix products, tile_batch(): jnp.einsum('kij,kjf->kif', chosen, everything[src_index], preferred_eleme...  7.47 us
    gather x4, local copies, waits for them, and re-layouts, pick_tiles(): chosen = tile_weight[jnp.maximum(tile_ids, 0)] * keep_mask[:, None, None]  6.93 us
  transfers between devices with their start and end apart: 4, of which 4 were waited for; matrix products, arithmetic and copies ran while one was open for 0% of the time, Pallas kernels for 0%

commit v1 on v0

--- a/solution.py
+++ b/solution.py
@@ -3,6 +3,18 @@
 import jax.numpy as jnp
 from jax import lax
 from jax.sharding import PartitionSpec as P
+
+
+def doubled_up(array, axis, dim):
+    ways, here = (lax.axis_size(axis), lax.axis_index(axis))
+    grown, reach = (array, 1)
+    while reach < ways:
+        theirs = lax.ppermute(grown, axis, [(d, d ^ reach) for d in range(ways)])
+        mine_first = jnp.concatenate([grown, theirs], axis=dim)
+        theirs_first = jnp.concatenate([theirs, grown], axis=dim)
+        grown = jnp.where(here & reach == 0, mine_first, theirs_first)
+        reach = 2 * reach
+    return grown
 
 
 def passed_along(value, axis, steps):
@@ -48,9 +60,7 @@
     scaled = (features.astype(jnp.float32) * src_scale[:, None]).astype(jnp.bfloat16)
     scaled = scaled.reshape(src_blocks, tile_len, feat_width)
     scaled_grads = (grad_out.astype(jnp.float32) * dst_scale[:, None]).astype(jnp.bfloat16)
-    grad_rows = lax.all_gather(scaled_grads, "col", axis=0, tiled=True).reshape(
-        dst_blocks, tile_len, feat_width
-    )
+    grad_rows = doubled_up(scaled_grads, "col", 0).reshape(dst_blocks, tile_len, feat_width)
 
     def pick_tiles(list_step):
         tile_ids = tile_list[list_step, 0]

time: 245 us -> 227 us (0.927)
  blocking collectives: 67.5 us -> 35.4 us
  waiting for transfers between devices: 65.3 us -> 83.4 us
  other arithmetic: 43.9 us -> 41.4 us
    all_gather x1 -> x0, blocking collectives: 31.5 us -> none  [local(): lax.all_gather(scaled_grads, 'col', axis=0, tiled=True)]
    ppermute x0 -> x3, waiting for transfers between devices: none -> 16.4 us  [doubled_up(): theirs = lax.ppermute(grown, axis, [(d, d ^ reach) for d in range(ways)])]
  transfers between devices with their start and end apart: 4 -> 7, of which waited for: 4 -> 6; matrix products, arithmetic and copies ran while one was open for 0% -> 1% of each run, Pallas kernels for 0% -> 0%
where the time goes in v1:
time: 227 us; the launch traced here: 226 us
  waiting for transfers between devices  83.4 us (37%)
  other arithmetic  41.4 us (18%)
  blocking collectives  35.4 us (16%)
  matrix products  25.9 us (11%)
  local copies, waits for them, and re-layouts  19.8 us (9%)
  between operations  15.6 us (7%)
  starting transfers between devices  3.99 us (2%)
    reduce_scatter x1, waiting for transfers between devices, local(): lax.psum_scatter(partial_value.reshape(dst_blocks * tile_len, feat_width)...  61.3 us
    unnamed x2, blocking collectives  29.1 us
    scatter-add x4, other arithmetic, backward_add(): return accum_total.at[src_index].add(products)  25.6 us
    dot_general x4, matrix products, backward_add(): jnp.einsum('kij,kif->kjf', chosen, rows[dst_index], preferred_element_typ...  17.9 us
    ppermute x3, waiting for transfers between devices, doubled_up(): theirs = lax.ppermute(grown, axis, [(d, d ^ reach) for d in range(ways)])  16.4 us
    scatter-add x4, other arithmetic, tile_batch(): return partial_value.at[dst_index].add(products)  8.78 us
    dot_general x4, matrix products, tile_batch(): jnp.einsum('kij,kjf->kif', chosen, everything[src_index], preferred_eleme...  7.47 us
    gather x4, local copies, waits for them, and re-layouts, pick_tiles(): chosen = tile_weight[jnp.maximum(tile_ids, 0)] * keep_mask[:, None, None]  6.94 us
  transfers between devices with their start and end apart: 7, of which 6 were waited for; matrix products, arithmetic and copies ran while one was open for 1% of the time, Pallas kernels for 0%

profile of v1, /device:TPU:0, one launch (start us, length us, event | category | flops | bytes accessed | tf_op | source)
XLA Modules:
  0.0 226.0 jit_solution(1540030039732060412)
XLA Ops:
  7.3 0.9 fusion.34
  8.6 2.3 convert_reduce_fusion
  11.1 23.2 %all-reduce.1 = f32[1024]{0:T(1024)S(1)} all-reduce(f32[1024]{0:T(1024)S(1)} %convolution_bitcast_fusion), channel_id=5, replica_groups=mesh['row'=4,'col'=8] {'col'}, use_global_device_ids=true, to_apply=%region_11.12.clone | all-reduce | flops 1024 | bytes 8192
  34.2 0.6 dynamic-slice.2
  36.1 3.9 %collective-permute-done.1 = bf16[128,256]{1,0:T(8,128)(2,1)S(1)} collective-permute-done((bf16[128,256]{1,0:T(8,128)(2,1)S(1)}, bf16[128,256]{1,0:T(8,128)(2,1)S(1)}, u32[]{:S(2)}, u32[]{:S(2)}) %collective-permute-start.1) | collective-permute-done | bytes 65568 | tf_op jit(solution)/shard_map/ppermute | solution.py:12
  40.1 0.6 dynamic-slice
  41.4 6.0 %all-reduce = f32[512]{0:T(512)S(1)} all-reduce(f32[512]{0:T(512)S(1)} %convolution_bitcast_fusion.1), channel_id=3, replica_groups=mesh['row'=4,'col'=8] {'row'}, use_global_device_ids=true, to_apply=%region_5.6.clone | all-reduce | flops 512 | bytes 4096
  47.6 1.7 gather_fusion.3
  49.3 12.5 %collective-permute-done.3 = bf16[512,256]{1,0:T(8,128)(2,1)S(1)} collective-permute-done((bf16[512,256]{1,0:T(8,128)(2,1)S(1)}, bf16[512,256]{1,0:T(8,128)(2,1)S(1)}, u32[]{:S(2)}, u32[]{:S(2)}) %collective-permute-start.3) | collective-permute-done | bytes 262176 | tf_op jit(solution)/shard_map/ppermute | solution.py:12
  62.1 2.0 gather_fusion.4
  64.1 5.0 %fusion.13 = f32[32,128,256]{2,1,0:T(8,128)} fusion(bf16[32,128,256]{2,1,0:T(8,128)(2,1)} %gather_fusion.4, bf16[32,128,128]{2,1,0:T(8,128)(2,1)} %gather_fusion.3, bf16[32]{0:T(256)(128)(2,1)S(1)} %fusion.26), kind=kOutput, calls=%fused_computation.41 | convolution fusion | flops 268959744 | bytes 7340096 | tf_op jit(solution)/shard_map/kij,kif->kjf/dot_general | solution.py:73
  69.0 49.5 %while.30 = (s32[]{:T(128)}, f32[1,128,256]{2,1,0:T(8,128)S(1)}, s32[4,3,32]{2,1,0:T(4,128)S(1)}, bf16[64,128,128]{2,1,0:T(8,128)(2,1)S(1)}, bf16[8,128,256]{2,1...) while((s32[]{:T(128)}, f32[1,128,256]{2,1,0:T(8,128)S(1)}, ...), condition=%wide.region_14.15_spmd.clone, body=%wide.region_12.14_spmd.clone.sunk | while | flops 270109056 | bytes 35530608 | solution.py:107
  69.1 1.7 gather_fusion.2
  70.9 0.7 gather_fusion.1
  71.6 4.3 %fusion.57 = f32[32,128,256]{2,1,0:T(8,128)} fusion(bf16[32,128,256]{2,1,0:T(8,128)(2,1)S(1)} %gather_fusion.1, bf16[32,128,128]{2,1,0:T(8,128)(2,1)} %gather_fusion.2, bf16[32]{0:T(256)(128)(2,1)S(1)} %fusion.56), kind=kOutput, calls=%fused_computation.17.clone.1 | convolution fusion | flops 268959744 | bytes 7340096 | tf_op jit(solution)/shard_map/while/body/eval_jaxpr/kij,kif->kjf/dot_general | solution.py:73
  75.9 6.4 %scatter_fusion.1 = f32[128,256,1]{1,0,2:T(8,128)S(1)} fusion(f32[128,256,1]{1,0,2:T(8,128)S(1)} %select_bitcast_fusion.2, s32[32]{0:T(128)S(1)} %fusion.54, f32[32,128,256]{2,1,0:T(8,128)} %fusion.57), kind=kCustom, calls=%fused_computation.6.clone.clone.1 | custom fusion | flops 1048576 | bytes 12583040 | tf_op jit(solution)/shard_map/while/body/eval_jaxpr/scatter-add | solution.py:76
  82.4 1.9 collective-permute-done
  84.5 1.7 gather_fusion.2
  86.2 0.7 gather_fusion.1
  86.9 4.3 %fusion.57 = f32[32,128,256]{2,1,0:T(8,128)} fusion(bf16[32,128,256]{2,1,0:T(8,128)(2,1)S(1)} %gather_fusion.1, bf16[32,128,128]{2,1,0:T(8,128)(2,1)} %gather_fusion.2, bf16[32]{0:T(256)(128)(2,1)S(1)} %fusion.56), kind=kOutput, calls=%fused_computation.17.clone.1 | convolution fusion | flops 268959744 | bytes 7340096 | tf_op jit(solution)/shard_map/while/body/eval_jaxpr/kij,kif->kjf/dot_general | solution.py:73
  91.2 6.4 %scatter_fusion.1 = f32[128,256,1]{1,0,2:T(8,128)S(1)} fusion(f32[128,256,1]{1,0,2:T(8,128)S(1)} %select_bitcast_fusion.2, s32[32]{0:T(128)S(1)} %fusion.54, f32[32,128,256]{2,1,0:T(8,128)} %fusion.57), kind=kCustom, calls=%fused_computation.6.clone.clone.1 | custom fusion | flops 1048576 | bytes 12583040 | tf_op jit(solution)/shard_map/while/body/eval_jaxpr/scatter-add | solution.py:76
  97.7 1.8 collective-permute-start
  99.5 1.9 collective-permute-done
  101.6 1.7 gather_fusion.2
  103.3 0.7 gather_fusion.1
  104.0 4.3 %fusion.57 = f32[32,128,256]{2,1,0:T(8,128)} fusion(bf16[32,128,256]{2,1,0:T(8,128)(2,1)S(1)} %gather_fusion.1, bf16[32,128,128]{2,1,0:T(8,128)(2,1)} %gather_fusion.2, bf16[32]{0:T(256)(128)(2,1)S(1)} %fusion.56), kind=kOutput, calls=%fused_computation.17.clone.1 | convolution fusion | flops 268959744 | bytes 7340096 | tf_op jit(solution)/shard_map/while/body/eval_jaxpr/kij,kif->kjf/dot_general | solution.py:73
  108.3 6.4 %scatter_fusion.1 = f32[128,256,1]{1,0,2:T(8,128)S(1)} fusion(f32[128,256,1]{1,0,2:T(8,128)S(1)} %select_bitcast_fusion.2, s32[32]{0:T(128)S(1)} %fusion.54, f32[32,128,256]{2,1,0:T(8,128)} %fusion.57), kind=kCustom, calls=%fused_computation.6.clone.clone.1 | custom fusion | flops 1048576 | bytes 12583040 | tf_op jit(solution)/shard_map/while/body/eval_jaxpr/scatter-add | solution.py:76
  114.8 1.8 collective-permute-start
  116.6 1.9 collective-permute-done
  118.6 6.3 %scatter_fusion.2 = f32[128,256,1]{1,0,2:T(8,128)S(1)} fusion(f32[128,256,1]{1,0,2:T(8,128)S(1)} %bitcast.83, s32[32]{0:T(128)S(1)} %fusion.27, f32[32,128,256]{2,1,0:T(8,128)} %fusion.13), kind=kCustom, calls=%fused_computation.7 | custom fusion | flops 1048576 | bytes 12583040 | tf_op jit(solution)/shard_map/scatter-add | solution.py:76
  124.9 0.7 fusion.16
  125.6 6.3 %all-gather = bf16[512,256]{1,0:T(8,128)(2,1)S(1)} all-gather(bf16[128,256]{1,0:T(8,128)(2,1)S(1)} %get-tuple-element.329), channel_id=2, replica_groups=mesh['row'=4,'col'=8] {'row'}, dimensions={0}, use_global_device_ids=true | all-gather | bytes 327680 | tf_op jit(solution)/shard_map/all_gather | solution.py:85
  132.0 23.5 %while.29 = (s32[]{:T(128)}, f32[8,128,256]{2,1,0:T(8,128)S(1)}, s32[64]{0:T(128)S(1)}, bf16[64,128,128]{2,1,0:T(8,128)(2,1)}, s32[64]{0:T(128)S(1)}, /*index=5*...) while((s32[]{:T(128)}, f32[8,128,256]{2,1,0:T(8,128)S(1)}, ...), condition=%wide.region_8.9_spmd, body=%wide.region_6.8_spmd.sunk | while | flops 135005296 | bytes 12063463 | solution.py:102
  132.2 1.6 gather_fusion
  133.8 1.9 fusion.51
  135.6 2.2 scatter_fusion
  138.0 1.6 gather_fusion
  139.6 1.9 fusion.51
  141.5 2.2 scatter_fusion
  143.9 1.6 gather_fusion
  145.5 1.9 fusion.51
  147.4 2.2 scatter_fusion
  149.8 1.6 gather_fusion
  151.4 1.9 fusion.51
  153.2 2.2 scatter_fusion
  155.4 0.8 convert_element_type.102
  156.3 61.3 %reduce-scatter.2.cloned.1.call-done = bf16[128,256]{1,0:T(8,128)(2,1)} async-done(((bf16[1024,256]{1,0:T(8,128)(2,1)}), bf16[128,256]{1,0:T(8,128)(2,1)}) %reduce-scatter.2.cloned.1.call-update) | async-done | bytes 65552 | tf_op jit(solution)/shard_map/reduce_scatter | solution.py:111
  217.6 1.6 multiply_convert_fusion.1
  (88 shorter events, 3.0 us)
Async XLA Ops:
  7.2 27.1 %copy-start.6 = (u32[32]{0:T(128)S(1)}, u32[32]{0:T(128)}, u32[]{:S(2)}) copy-start(u32[32]{0:T(128)} %constant.179) | copy-start | bytes 388
  7.2 32.9 %copy-start.5 = (u32[32]{0:T(128)S(1)}, u32[32]{0:T(128)}, u32[]{:S(2)}) copy-start(u32[32]{0:T(128)} %constant.175) | copy-start | bytes 388
  7.2 28.6 %copy-start.4 = (s32[4,3,32]{2,0,1:T(4,128)S(1)}, s32[4,3,32]{2,0,1:T(4,128)}, u32[]{:S(2)}) copy-start(s32[4,3,32]{2,0,1:T(4,128)} %param.11) | copy-start | bytes 4612
  7.2 40.4 %copy-start = (bf16[64,128,128]{2,1,0:T(8,128)(2,1)S(1)}, bf16[64,128,128]{2,1,0:T(8,128)(2,1)}, u32[]{:S(2)}) copy-start(bf16[64,128,128]{2,1,0:T(8,128)(2,1)} %param.10) | copy-start | bytes 6291460
  7.2 28.4 %copy-start.3 = (bf16[128,256]{1,0:T(8,128)(2,1)S(1)}, bf16[128,256]{1,0:T(8,128)(2,1)}, u32[]{:S(2)}) copy-start(bf16[128,256]{1,0:T(8,128)(2,1)} %param.9) | copy-start | bytes 196612
  7.2 210.4 %reduce-scatter.2.cloned.1.call-start = ((), (), s32[]{:S(2)}) async-start(), calls=%async_computation.1 | async-start | bytes 589824 | tf_op jit(solution)/shard_map/reduce_scatter | solution.py:111
  35.7 4.3 %collective-permute-start.1 = (bf16[128,256]{1,0:T(8,128)(2,1)S(1)}, bf16[128,256]{1,0:T(8,128)(2,1)S(1)}, u32[]{:S(2)}, u32[]{:S(2)}) collective-permute-start(bf16[128,256]{1,0:T(8,128)(2,1)S(1)} %multiply_convert_fusion), channel_id=1, source_target_pairs={{0,1},{1,0},{2,3},{3,2},{4,5},{5,4},{6,7},{7,6},{8,9},{9,8},{10,11... | collective-permute-start | bytes 196616 | tf_op jit(solution)/shard_map/ppermute | solution.py:12
  40.0 7.3 %collective-permute-start.2 = (bf16[256,256]{1,0:T(8,128)(2,1)S(1)}, bf16[256,256]{1,0:T(8,128)(2,1)S(1)}, u32[]{:S(2)}, u32[]{:S(2)}) collective-permute-start(bf16[256,256]{1,0:T(8,128)(2,1)S(1)} %maximum_select_fusion.2), channel_id=1, source_target_pairs={{0,2},{1,3},{2,0},{3,1},{4,6},{5,7},{6,4},{7,5},{8,10},{9,11},{10,... | collective-permute-start | bytes 393224 | tf_op jit(solution)/shard_map/ppermute | solution.py:12
  47.5 14.4 %collective-permute-start.3 = (bf16[512,256]{1,0:T(8,128)(2,1)S(1)}, bf16[512,256]{1,0:T(8,128)(2,1)S(1)}, u32[]{:S(2)}, u32[]{:S(2)}) collective-permute-start(bf16[512,256]{1,0:T(8,128)(2,1)S(1)} %maximum_select_fusion.1), channel_id=1, source_target_pairs={{0,4},{1,5},{2,6},{3,7},{4,0},{5,1},{6,2},{7,3},{8,12},{9,13},{10,... | collective-permute-start | bytes 786440 | tf_op jit(solution)/shard_map/ppermute | solution.py:12
  75.9 8.4 %copy-start.1 = (bf16[64,128,128]{2,1,0:T(8,128)(2,1)S(1)}, bf16[64,128,128]{2,1,0:T(8,128)(2,1)}, u32[]{:S(2)}) copy-start(bf16[64,128,128]{2,1,0:T(8,128)(2,1)} %get-tuple-element.478) | copy-start | bytes 6291460 | tf_op jit(solution)/shard_map/while
  82.3 2.0 collective-permute-start
  91.2 10.2 %copy-start.1 = (bf16[64,128,128]{2,1,0:T(8,128)(2,1)S(1)}, bf16[64,128,128]{2,1,0:T(8,128)(2,1)}, u32[]{:S(2)}) copy-start(bf16[64,128,128]{2,1,0:T(8,128)(2,1)} %get-tuple-element.478) | copy-start | bytes 6291460 | tf_op jit(solution)/shard_map/while
  97.7 3.7 %collective-permute-start = (bf16[1,128,256]{2,1,0:T(8,128)(2,1)S(1)}, bf16[1,128,256]{2,1,0:T(8,128)(2,1)S(1)}, u32[]{:S(2)}, u32[]{:S(2)}) collective-permute-start(bf16[1,128,256]{2,1,0:T(8,128)(2,1)S(1)} %convert_bitcast_fusion.2), channel_id=1, source_target_pairs={{0,24},{8,0},{16,8},{24,16},{1,25},{9,1},{17,9},{25,17},{2,26},{10... | collective-permute-start | bytes 196616 | tf_op jit(solution)/shard_map/while/body/eval_jaxpr/ppermute | solution.py:23
  108.3 10.2 %copy-start.1 = (bf16[64,128,128]{2,1,0:T(8,128)(2,1)S(1)}, bf16[64,128,128]{2,1,0:T(8,128)(2,1)}, u32[]{:S(2)}) copy-start(bf16[64,128,128]{2,1,0:T(8,128)(2,1)} %get-tuple-element.478) | copy-start | bytes 6291460 | tf_op jit(solution)/shard_map/while
  114.8 3.7 %collective-permute-start = (bf16[1,128,256]{2,1,0:T(8,128)(2,1)S(1)}, bf16[1,128,256]{2,1,0:T(8,128)(2,1)S(1)}, u32[]{:S(2)}, u32[]{:S(2)}) collective-permute-start(bf16[1,128,256]{2,1,0:T(8,128)(2,1)S(1)} %convert_bitcast_fusion.2), channel_id=1, source_target_pairs={{0,24},{8,0},{16,8},{24,16},{1,25},{9,1},{17,9},{25,17},{2,26},{10... | collective-permute-start | bytes 196616 | tf_op jit(solution)/shard_map/while/body/eval_jaxpr/ppermute | solution.py:23
  118.5 6.4 %copy-start.2 = (bf16[128,256]{1,0:T(8,128)(2,1)S(1)}, bf16[128,256]{1,0:T(8,128)(2,1)}, u32[]{:S(2)}) copy-start(bf16[128,256]{1,0:T(8,128)(2,1)} %param.8) | copy-start | bytes 196612
Sparse Core Ops, SparseCore 0:
  156.4 61.1 reduce-scatter.1
